TPU v7x, 32 devices: a whole 2x2x4 slice. The times are simulated.
32 devices in a mesh: tm: 4 (over z), sta: 8 (over y, x, core).
Axes of the slice: x: 2, y: 2, z: 4, core: 2. Of those that a mesh axis runs over, the one named last changes fastest.
Arguments:
- ray_basis: bfloat16 [4, 8192, 256], P('tm', 'sta'), may hold values from -0.13258252 to 0.13258252
- delays: bfloat16 [4, 8192], P('tm', 'sta'), may hold values from -24 to 24
- ray_station: int32 [4, 8192], P('tm', 'sta'), may hold values from 0 to 127, as said below
- ray_count: int32 [4, 8], P('tm', 'sta'), may hold values from 128 to 1024, as said below
- station_var: float32 [128], P('sta'), may hold values from 0.25 to 4
- decay_factor: float32 [4, 256], P('tm'), may hold values from 0.02 to 0.995, as said below
- mode_variance: float32 [256], replicated, may hold values from 0.3 to 3
- prior_mean: float32 [256], replicated, may hold values from -6 to 6
Outputs:
- smoothed: float32 [4, 256], P('tm')
Inputs may be any that keep to these rules, and one draw needn't show every extreme that they name: `ray_station`: each ray's station is one of the 16 stations of the station shard that holds the ray. `ray_count`: each entry is a multiple of 128; the live slots of a shard come first; some shard is full in every draw. `decay_factor`: each entry lies strictly between 0 and 1.
All inputs are finite; a program needn't handle non-finite values.
Results may differ from a plain program's by a relative error of at most 0.005.
Values sent between devices are 32-bit elements; how exact they have to be, the bound alone decides.
A program may use at most 64 MiB of HBM per device.

v0:
```python
import jax
import jax.numpy as jnp
from jax import lax
from jax.sharding import PartitionSpec as P

PRECISE = lax.Precision.HIGHEST


def passed_along(x, axis, by):
    devices = lax.axis_size(axis)
    pairs = [(i, i + by) for i in range(devices) if 0 <= i + by < devices]
    return lax.ppermute(x, axis, pairs)


def product(left, right):
    return jnp.dot(left, right, precision=PRECISE)


def spd_inverse(matrix):
    lower_factor = jnp.linalg.cholesky(matrix)
    identity = jnp.eye(matrix.shape[0], dtype=matrix.dtype)
    inverse = jax.scipy.linalg.cho_solve((lower_factor, True), identity)
    return 0.5 * (inverse + inverse.T)


def kalman_update(mean_prev, info_prev, decay_row, noise_row, information, drive_vector, is_first):
    inverse_noise = 1.0 / noise_row
    scaled = decay_row * inverse_noise
    identity = jnp.eye(noise_row.shape[0], dtype=jnp.float32)
    inner = jnp.where(is_first, identity, info_prev + jnp.diag(decay_row * scaled))
    kernel = spd_inverse(inner)
    pred_info = jnp.diag(inverse_noise) - jnp.where(
        is_first, 0.0, scaled[:, None] * kernel * scaled[None, :]
    )
    info_new = pred_info + information
    info_new = 0.5 * (info_new + info_new.T)
    target = product(pred_info, decay_row * mean_prev) + drive_vector
    factor = jnp.linalg.cholesky(info_new)
    mean_new = jax.scipy.linalg.cho_solve((factor, True), target)
    return (mean_new, info_new)


def run_filter(
    mean_prev, info_prev, first_index, decay_factor, process_noise, information, drive_vector
):
    is_first = first_index + 0 == 0
    mean_prev, info_prev = kalman_update(
        mean_prev,
        info_prev,
        decay_factor[0],
        process_noise[0],
        information[0],
        drive_vector[0],
        is_first,
    )
    filtered = [mean_prev]
    infos = [info_prev]
    return (jnp.stack(filtered), jnp.stack(infos))


def run_adjoint(adjoint, filtered, covariances, decay_factor, information, drive_vector):
    smoothed = []
    for position in reversed(range(decay_factor.shape[0])):
        smooth = filtered[position] + product(covariances[position], adjoint)
        adjoint = decay_factor[position] * (
            adjoint + drive_vector[position] - product(information[position], smooth)
        )
        smoothed.append(smooth)
    return (jnp.stack(smoothed[::-1]), adjoint)


def make_element(decay_row, noise_row, information, drive_vector, is_first, prior_mean):
    inverse_noise = 1.0 / noise_row
    covariance = spd_inverse(jnp.diag(inverse_noise) + information)
    scaled = decay_row * inverse_noise
    transition = covariance * scaled[None, :]
    offset = product(covariance, drive_vector)
    coupling = jnp.diag(scaled * decay_row) - scaled[:, None] * covariance * scaled[None, :]
    pulled = scaled * offset
    first_offset = offset + product(transition, prior_mean)
    return (
        jnp.where(is_first, 0.0, transition),
        jnp.where(is_first, first_offset, offset),
        covariance,
        jnp.where(is_first, 0.0, pulled),
        jnp.where(is_first, 0.0, coupling),
    )


def combine(earlier, later):
    early_map, early_offset, early_cov, early_pulled, early_coupling = earlier
    late_map, late_offset, late_cov, late_pulled, late_coupling = later
    identity = jnp.eye(early_cov.shape[0], dtype=early_cov.dtype)
    lower_factor = jnp.linalg.cholesky(early_cov)
    inner = identity + product(lower_factor.T, product(late_coupling, lower_factor))
    inner_factor = jnp.linalg.cholesky(0.5 * (inner + inner.T))
    solved = jax.scipy.linalg.solve_triangular(inner_factor, lower_factor.T, lower=True)
    gain = product(solved.T, solved)
    keeper = identity - product(gain, late_coupling)
    new_map = product(product(late_map, keeper), early_map)
    new_offset = (
        product(late_map, product(keeper, early_offset) + product(gain, late_pulled)) + late_offset
    )
    new_cov = product(product(late_map, gain), late_map.T) + late_cov
    reduced = late_coupling - product(late_coupling, product(gain, late_coupling))
    new_coupling = product(early_map.T, product(reduced, early_map)) + early_coupling
    new_pulled = (
        product(early_map.T, product(keeper.T, late_pulled - product(late_coupling, early_offset)))
        + early_pulled
    )
    return (
        new_map,
        new_offset,
        0.5 * (new_cov + new_cov.T),
        new_pulled,
        0.5 * (new_coupling + new_coupling.T),
    )


def shards(
    ray_basis, delays, ray_station, ray_count, station_var, decay_factor, mode_variance, prior_mean
):
    epochs_here, rays_here, state_width = ray_basis.shape
    stations_here = station_var.shape[0]
    tm_size = lax.axis_size("tm")
    tm_index = lax.axis_index("tm")
    first_index = tm_index * epochs_here
    local_station = ray_station - lax.axis_index("sta") * stations_here
    station_codes = jnp.arange(stations_here, dtype=jnp.int32)
    inverse_var = 1.0 / station_var
    matches = local_station[:, :, None] == station_codes[None, None, :]
    weight = jnp.sum(jnp.where(matches, inverse_var[None, None, :], 0.0), axis=2)
    slot_index = lax.broadcasted_iota(jnp.int32, (epochs_here, rays_here), 1)
    weight = jnp.where(slot_index < ray_count, weight, 0.0)
    weighted = (ray_basis * weight[:, :, None]).astype(jnp.bfloat16)
    info_part = jnp.einsum("ern,erm->enm", weighted, ray_basis, preferred_element_type=jnp.float32)
    drive_part = jnp.einsum("er,ern->en", delays, weighted, preferred_element_type=jnp.float32)
    information, drive_vector = lax.psum((info_part, drive_part), "sta")
    process_noise = (1.0 - decay_factor * decay_factor) * mode_variance[None, :]
    identity = jnp.eye(state_width, dtype=jnp.float32)
    levels = (tm_size - 1).bit_length()
    aggregate = None
    is_first = first_index + 0 == 0
    element = make_element(
        decay_factor[0], process_noise[0], information[0], drive_vector[0], is_first, prior_mean
    )
    aggregate = element
    for level_index in range(levels):
        distance = 1 << level_index
        received = passed_along(
            (aggregate[0], aggregate[1], aggregate[2], aggregate[3], aggregate[4]), "tm", distance
        )
        merged = combine(received, aggregate)
        is_valid = tm_index >= distance
        aggregate = jax.tree.map(
            lambda newer, older: jnp.where(is_valid, newer, older), merged, aggregate
        )
    previous = passed_along((aggregate[1], aggregate[2]), "tm", 1)
    mean_in = jnp.where(tm_index == 0, prior_mean, previous[0])
    info_in = spd_inverse(jnp.where(tm_index == 0, identity, previous[1]))
    filtered, filter_infos = run_filter(
        mean_in, info_in, first_index, decay_factor, process_noise, information, drive_vector
    )
    covariances = jnp.stack([spd_inverse(filter_infos[0])])

    def sweep(adjoint_in, kept):
        return run_adjoint(
            adjoint_in, filtered, covariances, decay_factor, information, drive_vector
        )

    def hold(adjoint_in, kept):
        return kept

    zero_vector = jnp.zeros((state_width,), jnp.float32)
    blank = (jnp.zeros((epochs_here, state_width), jnp.float32), zero_vector)
    kept = lax.cond(tm_index == tm_size - 1, sweep, hold, zero_vector, blank)

    def handback(turn, kept):
        received = passed_along(kept[1], "tm", -1)
        return lax.cond(tm_index == tm_size - 2 - turn, sweep, hold, received, kept)

    smoothed, _ = lax.fori_loop(0, tm_size - 1, handback, kept)
    return smoothed


def solution(mesh):
    placed = (
        P("tm", "sta", None),
        P("tm", "sta"),
        P("tm", "sta"),
        P("tm", "sta"),
        P("sta"),
        P("tm", None),
        P(),
        P(),
    )
    return jax.shard_map(
        shards, mesh=mesh, in_specs=placed, out_specs=P("tm", None), check_vma=False
    )
```

profile of v0, /device:TPU:0, one launch (start us, length us, event | category | flops | bytes accessed | tf_op | source)
XLA Modules:
  0.0 593.0 jit_solution(13307264366565452341)
XLA Ops:
  11.6 15.2 %psum.15 = f32[1,256]{1,0:T(1,128)S(1)} all-reduce(f32[1,256]{1,0:T(1,128)S(1)} %fusion.13), channel_id=1, replica_groups=mesh['tm'=4,'sta'=8] {'sta'}, use_global_device_ids=true, to_apply=%region_6.10 | all-reduce | flops 256 | bytes 2048 | tf_op jit(solution)/shard_map/psum | solution.py:138
  26.8 40.5 %all-reduce.3.cloned.1.call-done = f32[1,256,256]{1,2,0:T(8,128)} async-done(((f32[1,256,256]{1,2,0:T(8,128)}), f32[1,256,256]{1,2,0:T(8,128)}) %all-reduce.3.cloned.1.call-update) | async-done | bytes 262160 | tf_op jit(solution)/shard_map/psum | solution.py:138
  69.3 11.7 %cholesky.382 = f32[128,128]{1,0:T(8,128)S(1)} custom-call(f32[128,128]{1,0:T(8,128)S(1)} %cholesky.650), custom_call_target="Cholesky" | custom-call | tf_op jit(solution)/shard_map/jit(cholesky)/cholesky | solution.py:20
  91.4 11.7 %cholesky.399 = f32[128,128]{1,0:T(8,128)S(1)} custom-call(f32[128,128]{1,0:T(8,128)S(1)} %convolution_subtract_fusion.16), custom_call_target="Cholesky" | custom-call | tf_op jit(solution)/shard_map/jit(cholesky)/cholesky | solution.py:20
  109.3 20.0 %custom-call.42 = f32[2,128,128]{1,2,0:T(8,128)S(1)} custom-call(f32[2,128,128]{2,1,0:T(8,128)S(1)} %get-tuple-element.286), custom_call_target="InvertDiagBlocksLowerTriangular" | custom-call | tf_op jit(solution)/shard_map/jit(_cho_solve)/triangular_solve | solution.py:22
  147.6 11.7 %cholesky.416 = f32[128,128]{1,0:T(8,128)S(1)} custom-call(f32[128,128]{1,0:T(8,128)S(1)} %cholesky.653), custom_call_target="Cholesky" | custom-call | tf_op jit(solution)/shard_map/jit(cholesky)/cholesky | solution.py:94
  169.6 11.7 %cholesky.433 = f32[128,128]{1,0:T(8,128)S(1)} custom-call(f32[128,128]{1,0:T(8,128)S(1)} %slice_subtract_fusion.2), custom_call_target="Cholesky" | custom-call | tf_op jit(solution)/shard_map/jit(cholesky)/cholesky | solution.py:94
  185.5 11.9 %cholesky.450 = f32[128,128]{1,0:T(8,128)S(1)} custom-call(f32[128,128]{1,0:T(8,128)S(1)} %cholesky.656), custom_call_target="Cholesky" | custom-call | tf_op jit(solution)/shard_map/jit(cholesky)/cholesky | solution.py:96
  207.8 11.7 %cholesky.467 = f32[128,128]{1,0:T(8,128)S(1)} custom-call(f32[128,128]{1,0:T(8,128)S(1)} %convolution_subtract_fusion.15), custom_call_target="Cholesky" | custom-call | tf_op jit(solution)/shard_map/jit(cholesky)/cholesky | solution.py:96
  226.4 19.7 %custom-call.46 = f32[2,128,128]{1,2,0:T(8,128)S(1)} custom-call(f32[2,128,128]{2,1,0:T(8,128)S(1)} %get-tuple-element.288), custom_call_target="InvertDiagBlocksLowerTriangular" | custom-call | tf_op jit(solution)/shard_map/jit(_solve_triangular)/triangular_solve/custom-call.1 | solution.py:97
  261.9 11.7 %cholesky.484 = f32[128,128]{1,0:T(8,128)S(1)} custom-call(f32[128,128]{1,0:T(8,128)S(1)} %cholesky.659), custom_call_target="Cholesky" | custom-call | tf_op jit(solution)/shard_map/jit(cholesky)/cholesky | solution.py:94
  284.0 11.7 %cholesky.501 = f32[128,128]{1,0:T(8,128)S(1)} custom-call(f32[128,128]{1,0:T(8,128)S(1)} %slice_subtract_fusion.1), custom_call_target="Cholesky" | custom-call | tf_op jit(solution)/shard_map/jit(cholesky)/cholesky | solution.py:94
  300.1 11.7 %cholesky.518 = f32[128,128]{1,0:T(8,128)S(1)} custom-call(f32[128,128]{1,0:T(8,128)S(1)} %cholesky.662), custom_call_target="Cholesky" | custom-call | tf_op jit(solution)/shard_map/jit(cholesky)/cholesky | solution.py:96
  322.2 11.7 %cholesky.535 = f32[128,128]{1,0:T(8,128)S(1)} custom-call(f32[128,128]{1,0:T(8,128)S(1)} %convolution_subtract_fusion.14), custom_call_target="Cholesky" | custom-call | tf_op jit(solution)/shard_map/jit(cholesky)/cholesky | solution.py:96
  340.8 19.7 %custom-call.49 = f32[2,128,128]{1,2,0:T(8,128)S(1)} custom-call(f32[2,128,128]{2,1,0:T(8,128)S(1)} %get-tuple-element.289), custom_call_target="InvertDiagBlocksLowerTriangular" | custom-call | tf_op jit(solution)/shard_map/jit(_solve_triangular)/triangular_solve/custom-call.1 | solution.py:97
  374.5 11.7 %cholesky.552 = f32[128,128]{1,0:T(8,128)S(1)} custom-call(f32[128,128]{1,0:T(8,128)S(1)} %cholesky.665), custom_call_target="Cholesky" | custom-call | tf_op jit(solution)/shard_map/jit(cholesky)/cholesky | solution.py:20
  396.6 11.7 %cholesky.569 = f32[128,128]{1,0:T(8,128)S(1)} custom-call(f32[128,128]{1,0:T(8,128)S(1)} %slice_subtract_fusion), custom_call_target="Cholesky" | custom-call | tf_op jit(solution)/shard_map/jit(cholesky)/cholesky | solution.py:20
  415.1 19.8 %custom-call.51 = f32[2,128,128]{1,2,0:T(8,128)S(1)} custom-call(f32[2,128,128]{2,1,0:T(8,128)S(1)} %get-tuple-element.290), custom_call_target="InvertDiagBlocksLowerTriangular" | custom-call | tf_op jit(solution)/shard_map/jit(_cho_solve)/triangular_solve | solution.py:22
  437.2 11.7 %cholesky.586 = f32[128,128]{1,0:T(8,128)S(1)} custom-call(f32[128,128]{1,0:T(8,128)S(1)} %cholesky.668), custom_call_target="Cholesky" | custom-call | tf_op jit(solution)/shard_map/jit(cholesky)/cholesky | solution.py:20
  459.3 11.7 %cholesky.603 = f32[128,128]{1,0:T(8,128)S(1)} custom-call(f32[128,128]{1,0:T(8,128)S(1)} %convolution_subtract_fusion.13), custom_call_target="Cholesky" | custom-call | tf_op jit(solution)/shard_map/jit(cholesky)/cholesky | solution.py:20
  477.7 19.9 %custom-call.54 = f32[2,128,128]{1,2,0:T(8,128)S(1)} custom-call(f32[2,128,128]{2,1,0:T(8,128)S(1)} %get-tuple-element.292), custom_call_target="InvertDiagBlocksLowerTriangular" | custom-call | tf_op jit(solution)/shard_map/jit(_cho_solve)/triangular_solve | solution.py:22
  522.2 11.7 %cholesky.637 = f32[128,128]{1,0:T(8,128)S(1)} custom-call(f32[128,128]{1,0:T(8,128)S(1)} %convolution_subtract_fusion.12), custom_call_target="Cholesky" | custom-call | tf_op jit(solution)/shard_map/jit(cholesky)/cholesky | solution.py:20
  541.5 19.7 %custom-call.57 = f32[2,128,128]{1,2,0:T(8,128)S(1)} custom-call(f32[2,128,128]{2,1,0:T(8,128)S(1)} %get-tuple-element.294), custom_call_target="InvertDiagBlocksLowerTriangular" | custom-call | tf_op jit(solution)/shard_map/jit(_cho_solve)/triangular_solve | solution.py:22
  565.2 20.6 %while.40 = (s32[]{:T(128)}, f32[1,256]{1,0:T(1,128)}, f32[256]{0:T(256)S(1)}, s32[]{:T(128)}, f32[256,256]{1,0:T(8,128)S(1)}, /*index=5*/f32[256]{0:T(256)S(1)}...) while((s32[]{:T(128)}, f32[1,256]{1,0:T(1,128)}, ...), condition=%wide.region_12.16_spmd, body=%wide.region_9.15_spmd.sunk | while | flops 1573893 | bytes 545059 | solution.py:182
  (325 shorter events, 241.8 us)
Async XLA Ops:
  6.5 4.0 copy-start
  6.5 60.8 %all-reduce.3.cloned.1.call-start = ((), (), s32[]{:S(2)}) async-start(), calls=%async_computation | async-start | bytes 524288 | tf_op jit(solution)/shard_map/psum | solution.py:138
  6.5 0.7 copy-start.9
  6.5 1.3 copy-start.6
  8.0 2.5 copy-start.8
  10.5 0.7 copy-start.7
  10.9 0.7 copy-start.2
  68.3 1.0 copy-start.1
  131.7 0.7 copy-start.5
  132.7 13.1 %collective-permute-start.6 = (f32[256]{0:T(256)S(1)}, f32[256]{0:T(256)S(1)}, u32[]{:S(2)}, u32[]{:S(2)}) collective-permute-start(f32[256]{0:T(256)S(1)} %add_select_fusion.2), channel_id=1, source_target_pairs={{0,8},{8,16},{16,24},{1,9},{9,17},{17,25},{2,10},{10,18},{18,26},{... | collective-permute-start | bytes 3080 | tf_op jit(solution)/shard_map/ppermute | solution.py:12
  136.3 11.1 %collective-permute-start.1 = (f32[256,256]{0,1:T(8,128)S(1)}, f32[256,256]{0,1:T(8,128)S(1)}, u32[]{:S(2)}, u32[]{:S(2)}) collective-permute-start(f32[256,256]{0,1:T(8,128)S(1)} %get-tuple-element.432), channel_id=1, source_target_pairs={{0,8},{8,16},{16,24},{1,9},{9,17},{17,25},{2,10},{10,18},{18,26},{... | collective-permute-start | bytes 786440 | tf_op jit(solution)/shard_map/ppermute | solution.py:12
  139.7 110.9 %collective-permute-start.2 = (f32[256,256]{0,1:T(8,128)S(1)}, f32[256,256]{0,1:T(8,128)S(1)}, u32[]{:S(2)}, u32[]{:S(2)}) collective-permute-start(f32[256,256]{0,1:T(8,128)S(1)} %get-tuple-element.433), channel_id=1, source_target_pairs={{0,8},{8,16},{16,24},{1,9},{9,17},{17,25},{2,10},{10,18},{18,26},{... | collective-permute-start | bytes 786440 | tf_op jit(solution)/shard_map/ppermute | solution.py:12
  143.2 108.0 %collective-permute-start.4 = (f32[256,256]{1,0:T(8,128)S(1)}, f32[256,256]{1,0:T(8,128)}, u32[]{:S(2)}, u32[]{:S(2)}) collective-permute-start(f32[256,256]{1,0:T(8,128)S(1)} %copy.54), channel_id=1, source_target_pairs={{0,8},{8,16},{16,24},{1,9},{9,17},{17,25},{2,10},{10,18},{18,26},{... | collective-permute-start | bytes 786440 | tf_op jit(solution)/shard_map/ppermute | solution.py:12
  146.1 114.4 %collective-permute-start.8 = (f32[256]{0:T(256)S(1)}, f32[256]{0:T(256)S(1)}, u32[]{:S(2)}, u32[]{:S(2)}) collective-permute-start(f32[256]{0:T(256)S(1)} %get-tuple-element.415), channel_id=1, source_target_pairs={{0,8},{8,16},{16,24},{1,9},{9,17},{17,25},{2,10},{10,18},{18,26},{... | collective-permute-start | bytes 3080 | tf_op jit(solution)/shard_map/ppermute | solution.py:12
  253.5 8.2 %collective-permute-start.3 = (f32[256,256]{0,1:T(8,128)S(1)}, f32[256,256]{0,1:T(8,128)S(1)}, u32[]{:S(2)}, u32[]{:S(2)}) collective-permute-start(f32[256,256]{0,1:T(8,128)S(1)} %fusion.48), channel_id=1, source_target_pairs={{0,16},{8,24},{1,17},{9,25},{2,18},{10,26},{3,19},{11,27},{4,20},{... | collective-permute-start | bytes 786440 | tf_op jit(solution)/shard_map/ppermute | solution.py:12
  258.4 105.0 %collective-permute-start.7 = (f32[256]{0:T(256)S(1)}, f32[256]{0:T(256)S(1)}, u32[]{:S(2)}, u32[]{:S(2)}) collective-permute-start(f32[256]{0:T(256)S(1)} %add_select_fusion.1), channel_id=1, source_target_pairs={{0,16},{8,24},{1,17},{9,25},{2,18},{10,26},{3,19},{11,27},{4,20},{... | collective-permute-start | bytes 3080 | tf_op jit(solution)/shard_map/ppermute | solution.py:12
  364.8 9.5 %collective-permute-start.5 = (f32[256,256]{0,1:T(8,128)S(1)}, f32[256,256]{0,1:T(8,128)S(1)}, u32[]{:S(2)}, u32[]{:S(2)}) collective-permute-start(f32[256,256]{0,1:T(8,128)S(1)} %fusion.42), channel_id=1, source_target_pairs={{0,8},{8,16},{16,24},{1,9},{9,17},{17,25},{2,10},{10,18},{18,26},{... | collective-permute-start | bytes 786440 | tf_op jit(solution)/shard_map/ppermute | solution.py:12
  370.4 3.9 collective-permute-start.9
  565.2 6.7 %collective-permute-start = (f32[256]{0:T(256)S(1)}, f32[256]{0:T(256)S(1)}, u32[]{:S(2)}, u32[]{:S(2)}) collective-permute-start(f32[256]{0:T(256)S(1)} %get-tuple-element.826), channel_id=1, source_target_pairs={{8,0},{16,8},{24,16},{9,1},{17,9},{25,17},{10,2},{18,10},{26,18},{... | collective-permute-start | bytes 3080 | tf_op jit(solution)/shard_map/while/body/eval_jaxpr/ppermute | solution.py:12
  571.9 5.7 collective-permute-start
  577.6 7.3 %collective-permute-start = (f32[256]{0:T(256)S(1)}, f32[256]{0:T(256)S(1)}, u32[]{:S(2)}, u32[]{:S(2)}) collective-permute-start(f32[256]{0:T(256)S(1)} %get-tuple-element.826), channel_id=1, source_target_pairs={{8,0},{16,8},{24,16},{9,1},{17,9},{25,17},{10,2},{18,10},{26,18},{... | collective-permute-start | bytes 3080 | tf_op jit(solution)/shard_map/while/body/eval_jaxpr/ppermute | solution.py:12
  585.1 0.6 copy-start.4
Sparse Core Ops, SparseCore 0:
  10.6 56.6 all-reduce.2
where the time goes:
time: 602 us; the launch traced here: 593 us
  other arithmetic  398 us (66%)
  waiting for transfers between devices  58.3 us (10%)
  starting transfers between devices  32.2 us (5%)
  local copies, waits for them, and re-layouts  31.3 us (5%)
  matrix products  31.2 us (5%)
  between operations  26.2 us (4%)
  blocking collectives  15.2 us (3%)
    another operation x27, other arithmetic, spd_inverse(): lower_factor = jnp.linalg.cholesky(matrix)  138 us
    another operation x13, other arithmetic, spd_inverse(): inverse = jax.scipy.linalg.cho_solve((lower_factor, True), identity)  79.6 us
    another operation x14, other arithmetic, combine(): inner_factor = jnp.linalg.cholesky(0.5 * (inner + inner.T))  69.4 us
    another operation x14, other arithmetic, combine(): lower_factor = jnp.linalg.cholesky(early_cov)  69.3 us
    psum x1, waiting for transfers between devices, shards(): information, drive_vector = lax.psum((info_part, drive_part), 'sta')  40.5 us
    another operation x4, other arithmetic, combine(): jax.scipy.linalg.solve_triangular(inner_factor, lower_factor.T, lower=True)  39.4 us
    ppermute x12, starting transfers between devices, passed_along(): return lax.ppermute(x, axis, pairs)  32.2 us
    ppermute x12, waiting for transfers between devices, passed_along(): return lax.ppermute(x, axis, pairs)  17.7 us
  transfers between devices with their start and end apart: 13, of which 6 were waited for; matrix products, arithmetic and copies ran while one was open for 34% of the time, Pallas kernels for 0%

commit v1 on v0

v1 whole, which is shorter than its diff:
```python
import functools

import jax
import jax.numpy as jnp
from jax import lax
from jax.experimental import pallas as pl
from jax.experimental.pallas import tpu as pltpu
from jax.sharding import PartitionSpec as P

MESH = pl.DeviceIdType.MESH
CORES = 2
TOL = 1e-10
STEPS_PER_CHECK = 4
MAX_CHECKS = 500


def loop(n, body):
    if n <= 16:
        for i in range(n):
            body(i)
    else:
        def step(i, carry):
            body(i)
            return carry

        lax.fori_loop(0, n, step, 0)


def shard_rows(half, shards):
    rows = 3 * half + 2 * (2 * half // 128)
    return -(-rows // (8 * shards)) * 8


def exchange(
    tm_size, sta_size, rows, half,
    basis_ref, delay_ref, station_ref, count_ref, var_ref, decay_ref, out_ref,
    part, landed, rs_send, rs_recv, z_send, plane_send, core_send, gather_recv,
):
    tm = lax.axis_index("tm")
    sta = lax.axis_index("sta")
    core = sta % CORES
    chip = sta // CORES
    chips = sta_size // CORES

    barrier = pltpu.get_barrier_semaphore()

    def greet_plane(i):
        peer = (sta + 1 + i) % sta_size
        pl.semaphore_signal(barrier, inc=1, device_id=(tm, peer), device_id_type=MESH)

    def greet_column(i):
        peer = (tm + 1 + i) % tm_size
        pl.semaphore_signal(barrier, inc=1, device_id=(peer, sta), device_id_type=MESH)

    loop(sta_size - 1, greet_plane)
    loop(tm_size - 1, greet_column)

    rays = basis_ref.shape[1]
    width = 2 * half
    groups = rays // 128
    local = station_ref[...] - sta * var_ref.shape[0]
    slots = lax.broadcasted_iota(jnp.int32, (1, rays), 1)
    weight = jnp.zeros((1, rays), jnp.float32)
    for s in range(var_ref.shape[0]):
        value = jnp.full((1, rays), var_ref[s], jnp.float32)
        weight = jnp.where(local == s, 1.0 / value, weight)
    weight = jnp.where(slots < count_ref[0, 0], weight, 0.0)
    square = jnp.concatenate(
        [weight[:, g * 128 : (g + 1) * 128] for g in range(groups)]
        + [jnp.zeros((128 - groups, 128), jnp.float32)],
        axis=0,
    )
    columns = square.T
    weighted = jnp.concatenate(
        [
            (basis_ref[0, g * 128 : (g + 1) * 128, :].astype(jnp.float32) * columns[:, g : g + 1])
            for g in range(groups)
        ],
        axis=0,
    ).astype(jnp.bfloat16)
    basis = basis_ref[0]
    outer = (((0,), (0,)), ((), ()))
    left = lax.dot_general(
        weighted, basis[:, :half], outer, preferred_element_type=jnp.float32
    )
    corner = lax.dot_general(
        weighted[:, half:], basis[:, half:], outer, preferred_element_type=jnp.float32
    )
    drive = jnp.dot(delay_ref[...], weighted, preferred_element_type=jnp.float32)
    keep = jnp.where(jnp.full((1, width), sta, jnp.int32) == 0, decay_ref[...], 0.0)
    tail = [drive[:, i * half : (i + 1) * half] for i in range(2)]
    tail += [keep[:, i * half : (i + 1) * half] for i in range(2)]
    pad = sta_size * rows - 3 * half - 4
    flat = jnp.concatenate(
        [left, corner] + tail + [jnp.zeros((pad, half), jnp.float32)], axis=0
    )
    for s in range(sta_size):
        part[s] = flat[s * rows : (s + 1) * rows]

    pl.semaphore_wait(barrier, sta_size + tm_size - 2)

    def scatter(i):
        peer = (sta + 1 + i) % sta_size
        return pltpu.make_async_remote_copy(
            src_ref=part.at[peer], dst_ref=landed.at[sta],
            send_sem=rs_send.at[i], recv_sem=rs_recv.at[sta],
            device_id=(tm, peer), device_id_type=MESH,
        )

    def scattered(i):
        peer = (sta + 1 + i) % sta_size
        return pltpu.make_async_remote_copy(
            src_ref=part.at[peer], dst_ref=landed.at[peer],
            send_sem=rs_send.at[i], recv_sem=rs_recv.at[peer],
            device_id=(tm, peer), device_id_type=MESH,
        )

    loop(sta_size - 1, lambda i: scatter(i).start())
    loop(sta_size - 1, lambda i: scattered(i).wait_recv())
    total = part[sta]
    if sta_size <= 16:
        for i in range(sta_size - 1):
            total = total + landed[(sta + 1 + i) % sta_size]
    else:
        total = lax.fori_loop(
            0, sta_size - 1, lambda i, t: t + landed[(sta + 1 + i) % sta_size], total
        )
    out_ref[tm, sta] = total

    def slot_copy(z, s, send_sem, device):
        return pltpu.make_async_remote_copy(
            src_ref=out_ref.at[z, s], dst_ref=out_ref.at[z, s],
            send_sem=send_sem, recv_sem=gather_recv.at[z, s],
            device_id=device, device_id_type=MESH,
        )

    def column_copy(i):
        return slot_copy(tm, sta, z_send.at[i], ((tm + 1 + i) % tm_size, sta))

    def plane_copy(z, i):
        peer = ((chip + 1 + i) % chips) * CORES + core
        return slot_copy(z, sta, plane_send.at[z, i], (tm, peer))

    def core_copy(z, c):
        return slot_copy(z, c * CORES + core, core_send.at[z, c], (tm, chip * CORES + 1 - core))

    def spread(z):
        loop(chips - 1, lambda i: plane_copy(z, i).start())
        core_copy(z, chip).start()

    loop(tm_size - 1, lambda i: column_copy(i).start())
    spread(tm)

    def relay(i):
        z = (tm + 1 + i) % tm_size
        slot_copy(z, sta, core_send.at[z, chip], (tm, sta)).wait_recv()
        spread(z)

    loop(tm_size - 1, relay)

    def share(j):
        z = (tm + j) % tm_size

        def one(i):
            c = (chip + 1 + i) % chips
            slot_copy(z, c * CORES + core, core_send.at[z, c], (tm, sta)).wait_recv()
            core_copy(z, c).start()

        loop(chips - 1, one)

    loop(tm_size, share)

    def collect(z):
        def one(c):
            slot_copy(
                z, c * CORES + 1 - core, core_send.at[z, c], (tm, sta)
            ).wait_recv()

        loop(chips, one)

    loop(tm_size, collect)
    loop(sta_size - 1, lambda i: scatter(i).wait_send())
    loop(tm_size - 1, lambda i: column_copy(i).wait_send())

    def drain(z):
        loop(chips - 1, lambda i: plane_copy(z, i).wait_send())
        loop(chips, lambda c: core_copy(z, c).wait_send())

    loop(tm_size, drain)


def total_of(rows):
    acc = rows[0]
    for row in rows[1:]:
        acc = acc + row
    return jnp.sum(acc, axis=1, keepdims=True)


def solve(epochs, half, packed_ref, variance_ref, prior_ref, out_ref, table):
    width = 2 * half
    tm = lax.axis_index("tm")
    row_id = lax.broadcasted_iota(jnp.int32, (half, half), 0)
    col_id = lax.broadcasted_iota(jnp.int32, (half, half), 1)
    diagonal = row_id == col_id
    variance = variance_ref[...]
    decay, drive, info_diag = [], [], []
    for e in range(epochs):
        upper = packed_ref[e, :half]
        lower = packed_ref[e, half : 2 * half]
        corner = packed_ref[e, 2 * half : 3 * half]
        matrix = jnp.concatenate(
            [
                jnp.concatenate([upper, lower.T], axis=1),
                jnp.concatenate([lower, corner], axis=1),
            ],
            axis=0,
        )
        high = matrix.astype(jnp.bfloat16)
        table[e, :width] = high
        table[e, width:] = (matrix - high.astype(jnp.float32)).astype(jnp.bfloat16)
        info_diag.append(
            jnp.concatenate(
                [
                    jnp.sum(jnp.where(diagonal, block, 0.0), axis=0, keepdims=True)
                    for block in (upper, corner)
                ],
                axis=1,
            )
        )
        tail = packed_ref[e, 3 * half : 3 * half + 8]
        drive.append(jnp.concatenate([tail[0:1], tail[1:2]], axis=1))
        decay.append(jnp.concatenate([tail[2:3], tail[3:4]], axis=1))
    inverse_noise = [1.0 / ((1.0 - d * d) * variance) for d in decay]
    off = [-decay[e] * inverse_noise[e] for e in range(epochs)]
    main = []
    for e in range(epochs):
        value = inverse_noise[e]
        if e + 1 < epochs:
            value = value + decay[e + 1] * decay[e + 1] * inverse_noise[e + 1]
        main.append(value)
    target = list(drive)
    target[0] = target[0] + inverse_noise[0] * (decay[0] * prior_ref[...])

    pivot_inverse, ratio = [], []
    for e in range(epochs):
        pivot = main[e] + info_diag[e]
        if e:
            ratio.append(off[e] * pivot_inverse[-1])
            pivot = pivot - ratio[-1] * off[e]
        pivot_inverse.append(1.0 / pivot)

    def precondition(r):
        y = [r[0]]
        for e in range(1, epochs):
            y.append(r[e] - ratio[e - 1] * y[-1])
        z = [None] * epochs
        z[-1] = y[-1] * pivot_inverse[-1]
        for e in range(epochs - 2, -1, -1):
            z[e] = y[e] * pivot_inverse[e] - ratio[e] * z[e + 1]
        return z

    pick = lax.broadcasted_iota(jnp.int32, (8, width), 0)

    def apply(p):
        result = []
        for e in range(epochs):
            first = p[e].astype(jnp.bfloat16).astype(jnp.float32)
            rest = p[e] - first
            second = rest.astype(jnp.bfloat16).astype(jnp.float32)
            third = rest - second
            stacked = jnp.where(
                pick == 0, first, jnp.where(pick == 1, second, jnp.where(pick == 2, third, 0.0))
            ).astype(jnp.bfloat16)
            both = jnp.concatenate([stacked, stacked], axis=1)
            product = jnp.dot(both, table[e], preferred_element_type=jnp.float32)
            value = main[e] * p[e] + jnp.sum(product, axis=0, keepdims=True)
            if e:
                value = value + off[e] * p[e - 1]
            if e + 1 < epochs:
                value = value + off[e + 1] * p[e + 1]
            result.append(value)
        return result

    tiny = 1e-30
    zero = [jnp.zeros((1, width), jnp.float32)] * epochs
    first_z = precondition(target)
    first_rz = total_of([a * b for a, b in zip(target, first_z)])
    goal = TOL * first_rz

    def body(carry):
        count, _, x, r, p, rz = carry
        x, r, p = list(x), list(r), list(p)
        for _ in range(STEPS_PER_CHECK):
            q = apply(p)
            bend = total_of([a * b for a, b in zip(p, q)])
            alpha = rz / jnp.maximum(bend, tiny)
            x = [a + alpha * b for a, b in zip(x, p)]
            r = [a - alpha * b for a, b in zip(r, q)]
            z = precondition(r)
            new = total_of([a * b for a, b in zip(r, z)])
            beta = new / jnp.maximum(rz, tiny)
            p = [a + beta * b for a, b in zip(z, p)]
            rz = new
        going = jnp.max((rz > goal).astype(jnp.int32)) > 0
        return (count + 1, going, tuple(x), tuple(r), tuple(p), rz)

    start = (
        jnp.int32(0), jnp.max((first_rz > tiny).astype(jnp.int32)) > 0,
        tuple(zero), tuple(target), tuple(first_z), first_rz,
    )
    final = lax.while_loop(lambda c: jnp.logical_and(c[1], c[0] < MAX_CHECKS), body, start)
    chosen = final[2][0]
    for e in range(1, epochs):
        chosen = jnp.where(tm == e, final[2][e], chosen)
    out_ref[...] = chosen


def shards(
    ray_basis, delays, ray_station, ray_count, station_var, decay_factor, mode_variance, prior_mean
):
    tm_size = lax.axis_size("tm")
    sta_size = lax.axis_size("sta")
    width = ray_basis.shape[2]
    half = width // 2
    rows = shard_rows(half, sta_size)
    chips = sta_size // CORES
    vmem = pl.BlockSpec(memory_space=pltpu.VMEM)
    smem = pl.BlockSpec(memory_space=pltpu.SMEM)
    dma = pltpu.SemaphoreType.DMA
    packed = pl.pallas_call(
        functools.partial(exchange, tm_size, sta_size, rows, half),
        out_shape=jax.ShapeDtypeStruct((tm_size, sta_size, rows, half), jnp.float32),
        in_specs=[vmem, vmem, vmem, smem, smem, vmem],
        out_specs=vmem,
        scratch_shapes=[
            pltpu.VMEM((sta_size, rows, half), jnp.float32),
            pltpu.VMEM((sta_size, rows, half), jnp.float32),
            dma((sta_size - 1,)),
            dma((sta_size,)),
            dma((tm_size - 1,)),
            dma((tm_size, chips - 1)),
            dma((tm_size, chips)),
            dma((tm_size, sta_size)),
        ],
        compiler_params=pltpu.CompilerParams(collective_id=0, has_side_effects=True),
        name="exchange",
    )(ray_basis, delays, ray_station, ray_count, station_var, decay_factor)
    packed = packed.reshape(tm_size, sta_size * rows, half)
    return pl.pallas_call(
        functools.partial(solve, tm_size, half),
        out_shape=jax.ShapeDtypeStruct((1, width), jnp.float32),
        in_specs=[vmem, vmem, vmem],
        out_specs=vmem,
        scratch_shapes=[pltpu.VMEM((tm_size, 2 * width, width), jnp.bfloat16)],
        name="solve",
    )(packed, mode_variance.reshape(1, width), prior_mean.reshape(1, width))


def solution(mesh):
    placed = (
        P("tm", "sta", None),
        P("tm", "sta"),
        P("tm", "sta"),
        P("tm", "sta"),
        P("sta"),
        P("tm", None),
        P(),
        P(),
    )
    return jax.shard_map(
        shards, mesh=mesh, in_specs=placed, out_specs=P("tm", None), check_vma=False
    )
```

time: 602 us -> 29.5 us (0.05); the launches traced: 593 us -> 29.3 us
  other arithmetic: 398 us -> 0 us
  waiting for transfers between devices: 58.3 us -> 0 us
  starting transfers between devices: 32.2 us -> 0 us
  local copies, waits for them, and re-layouts: 31.3 us -> 0 us
  matrix products: 31.2 us -> 0 us
  Pallas kernels: 0 us -> 28.6 us
  between operations: 26.2 us -> 0.66 us
  blocking collectives: 15.2 us -> 0 us
    another operation x73 -> x0, other arithmetic: 396 us -> none  [the longest x27 138 us: spd_inverse(): lower_factor = jnp.linalg.cholesky(matrix)]
    psum x1 -> x0, waiting for transfers between devices: 40.5 us -> none  [shards(): information, drive_vector = lax.psum((info_part, drive_part), 'sta')]
    ppermute x12 -> x0, starting transfers between devices: 32.2 us -> none  [passed_along(): return lax.ppermute(x, axis, pairs)]
    pallas_call x0 -> x2, Pallas kernels: none -> 28.6 us  [the longest x1 21.2 us: shards(): pl.pallas_call(functools.partial(exchange, tm_size, sta_size, rows, half)...]
    another operation x72 -> x0, local copies, waits for them, and re-layouts: 25 us -> none  [the longest x39 16.5 us: spd_inverse(): inverse = jax.scipy.linalg.cho_solve((lower_factor, True), identity)]
    ppermute x12 -> x0, waiting for transfers between devices: 17.7 us -> none  [passed_along(): return lax.ppermute(x, axis, pairs)]
    dot_general x33 -> x0, matrix products: 16.9 us -> none  [the longest x31 14.1 us: product(): return jnp.dot(left, right, precision=PRECISE)]
    psum x1 -> x0, blocking collectives: 15.2 us -> none  [shards(): information, drive_vector = lax.psum((info_part, drive_part), 'sta')]
  transfers between devices with their start and end apart: 13 -> 0, of which waited for: 6 -> 0; matrix products, arithmetic and copies ran while one was open for 34% -> 0% of each run, Pallas kernels for 0% -> 0%
where the time goes in v1:
time: 29.5 us; the launch traced here: 29.3 us
  Pallas kernels  28.6 us (97%)
  between operations  0.66 us (2%)
    pallas_call x1, Pallas kernels, shards(): pl.pallas_call(functools.partial(exchange, tm_size, sta_size, rows, half)...  21.2 us
    pallas_call x1, Pallas kernels, shards(): pl.pallas_call(functools.partial(solve, tm_size, half), out_shape=jax.Sha...  7.46 us

profile of v1, /device:TPU:0, one launch (start us, length us, event | category | flops | bytes accessed | tf_op | source)
XLA Modules:
  0.0 29.3 jit_solution(2859487403341109046)
XLA Ops:
  0.7 21.2 %exchange.1 = f32[4,8,56,128]{3,2,1,0:T(8,128)} custom-call(bf16[1,1024,256]{2,1,0:T(8,128)(2,1)} %basis_ref.1, bf16[1,1024]{1,0:T(2,128)(2,1)} %delay_ref.1, s32[1,1024]{1,0:T(1,128)} %station_ref.1, s32[1,1]{1,0:T(1,128)S(6)} %copy.9.count_ref, f32[16]{0:T(128)} %var_ref.1, f32[1,256]{1,0:T(1,128)} %decay_ref.1), custom_call_target="tpu_custom_call" | custom-call | tf_op jit(solution)/shard_map/exchange/pallas_call | solution.py:330
  21.8 7.5 %solve.1 = f32[1,256]{1,0:T(1,128)} custom-call(f32[4,448,128]{2,1,0:T(8,128)} %bitcast.3, f32[1,256]{1,0:T(1,128)} %bitcast.4, f32[1,256]{1,0:T(1,128)} %bitcast.5), custom_call_target="tpu_custom_call" | custom-call | tf_op jit(solution)/shard_map/solve/pallas_call | solution.py:349

commit v2 on v1

--- a/solution.py
+++ b/solution.py
@@ -9,9 +9,11 @@
 
 MESH = pl.DeviceIdType.MESH
 CORES = 2
-TOL = 1e-10
-STEPS_PER_CHECK = 4
-MAX_CHECKS = 500
+TOL = 2e-8
+FIRST_STEPS = 7
+STEPS_PER_CHECK = 3
+MAX_CHECKS = 700
+VMEM_BYTES = 24 << 20
 
 
 def loop(n, body):
@@ -27,7 +29,7 @@
 
 
 def shard_rows(half, shards):
-    rows = 3 * half + 2 * (2 * half // 128)
+    rows = 2 * half + 5
     return -(-rows // (8 * shards)) * 8
 
 
@@ -60,11 +62,10 @@
     groups = rays // 128
     local = station_ref[...] - sta * var_ref.shape[0]
     slots = lax.broadcasted_iota(jnp.int32, (1, rays), 1)
-    weight = jnp.zeros((1, rays), jnp.float32)
+    noise = jnp.ones((1, rays), jnp.float32)
     for s in range(var_ref.shape[0]):
-        value = jnp.full((1, rays), var_ref[s], jnp.float32)
-        weight = jnp.where(local == s, 1.0 / value, weight)
-    weight = jnp.where(slots < count_ref[0, 0], weight, 0.0)
+        noise = jnp.where(local == s, var_ref[s], noise)
+    weight = jnp.where(slots < count_ref[0, 0], 1.0 / noise, 0.0)
     square = jnp.concatenate(
         [weight[:, g * 128 : (g + 1) * 128] for g in range(groups)]
         + [jnp.zeros((128 - groups, 128), jnp.float32)],
@@ -88,11 +89,15 @@
     )
     drive = jnp.dot(delay_ref[...], weighted, preferred_element_type=jnp.float32)
     keep = jnp.where(jnp.full((1, width), sta, jnp.int32) == 0, decay_ref[...], 0.0)
-    tail = [drive[:, i * half : (i + 1) * half] for i in range(2)]
+    row_id = lax.broadcasted_iota(jnp.int32, (half, half), 0)
+    col_id = lax.broadcasted_iota(jnp.int32, (half, half), 1)
+    mixed = jnp.where(row_id >= col_id, left[:half], corner)
+    tail = [jnp.sum(jnp.where(row_id == col_id, corner, 0.0), axis=0, keepdims=True)]
+    tail += [drive[:, i * half : (i + 1) * half] for i in range(2)]
     tail += [keep[:, i * half : (i + 1) * half] for i in range(2)]
-    pad = sta_size * rows - 3 * half - 4
+    pad = sta_size * rows - 2 * half - 5
     flat = jnp.concatenate(
-        [left, corner] + tail + [jnp.zeros((pad, half), jnp.float32)], axis=0
+        [mixed, left[half:]] + tail + [jnp.zeros((pad, half), jnp.float32)], axis=0
     )
     for s in range(sta_size):
         part[s] = flat[s * rows : (s + 1) * rows]
@@ -205,9 +210,14 @@
     variance = variance_ref[...]
     decay, drive, info_diag = [], [], []
     for e in range(epochs):
-        upper = packed_ref[e, :half]
+        mixed = packed_ref[e, :half]
         lower = packed_ref[e, half : 2 * half]
-        corner = packed_ref[e, 2 * half : 3 * half]
+        tail = packed_ref[e, 2 * half : 2 * half + 8]
+        flipped = mixed.T
+        upper = jnp.where(row_id >= col_id, mixed, flipped)
+        corner = jnp.where(
+            row_id < col_id, mixed, jnp.where(diagonal, tail[0:1], flipped)
+        )
         matrix = jnp.concatenate(
             [
                 jnp.concatenate([upper, lower.T], axis=1),
@@ -220,16 +230,12 @@
         table[e, width:] = (matrix - high.astype(jnp.float32)).astype(jnp.bfloat16)
         info_diag.append(
             jnp.concatenate(
-                [
-                    jnp.sum(jnp.where(diagonal, block, 0.0), axis=0, keepdims=True)
-                    for block in (upper, corner)
-                ],
+                [jnp.sum(jnp.where(diagonal, mixed, 0.0), axis=0, keepdims=True), tail[0:1]],
                 axis=1,
             )
         )
-        tail = packed_ref[e, 3 * half : 3 * half + 8]
-        drive.append(jnp.concatenate([tail[0:1], tail[1:2]], axis=1))
-        decay.append(jnp.concatenate([tail[2:3], tail[3:4]], axis=1))
+        drive.append(jnp.concatenate([tail[1:2], tail[2:3]], axis=1))
+        decay.append(jnp.concatenate([tail[3:4], tail[4:5]], axis=1))
     inverse_noise = [1.0 / ((1.0 - d * d) * variance) for d in decay]
     off = [-decay[e] * inverse_noise[e] for e in range(epochs)]
     main = []
@@ -287,10 +293,9 @@
     first_rz = total_of([a * b for a, b in zip(target, first_z)])
     goal = TOL * first_rz
 
-    def body(carry):
-        count, _, x, r, p, rz = carry
-        x, r, p = list(x), list(r), list(p)
-        for _ in range(STEPS_PER_CHECK):
+    def advance(state, steps):
+        x, r, p, rz = list(state[0]), list(state[1]), list(state[2]), state[3]
+        for _ in range(steps):
             q = apply(p)
             bend = total_of([a * b for a, b in zip(p, q)])
             alpha = rz / jnp.maximum(bend, tiny)
@@ -301,17 +306,25 @@
             beta = new / jnp.maximum(rz, tiny)
             p = [a + beta * b for a, b in zip(z, p)]
             rz = new
-        going = jnp.max((rz > goal).astype(jnp.int32)) > 0
-        return (count + 1, going, tuple(x), tuple(r), tuple(p), rz)
-
-    start = (
-        jnp.int32(0), jnp.max((first_rz > tiny).astype(jnp.int32)) > 0,
-        tuple(zero), tuple(target), tuple(first_z), first_rz,
-    )
-    final = lax.while_loop(lambda c: jnp.logical_and(c[1], c[0] < MAX_CHECKS), body, start)
-    chosen = final[2][0]
+        return tuple(x), tuple(r), tuple(p), rz
+
+    def going(rz):
+        return jnp.max((rz > goal).astype(jnp.int32)) > 0
+
+    def body(carry):
+        count, _, state = carry
+        state = advance(state, STEPS_PER_CHECK)
+        return count + 1, going(state[3]), state
+
+    state = advance((zero, target, first_z, first_rz), FIRST_STEPS)
+    final = lax.while_loop(
+        lambda c: jnp.logical_and(c[1], c[0] < MAX_CHECKS),
+        body,
+        (jnp.int32(0), going(state[3]), state),
+    )[2][0]
+    chosen = final[0]
     for e in range(1, epochs):
-        chosen = jnp.where(tm == e, final[2][e], chosen)
+        chosen = jnp.where(tm == e, final[e], chosen)
     out_ref[...] = chosen
 
 
@@ -342,7 +355,9 @@
             dma((tm_size, chips)),
             dma((tm_size, sta_size)),
         ],
-        compiler_params=pltpu.CompilerParams(collective_id=0, has_side_effects=True),
+        compiler_params=pltpu.CompilerParams(
+            collective_id=0, has_side_effects=True, vmem_limit_bytes=VMEM_BYTES
+        ),
         name="exchange",
     )(ray_basis, delays, ray_station, ray_count, station_var, decay_factor)
     packed = packed.reshape(tm_size, sta_size * rows, half)
@@ -352,6 +367,7 @@
         in_specs=[vmem, vmem, vmem],
         out_specs=vmem,
         scratch_shapes=[pltpu.VMEM((tm_size, 2 * width, width), jnp.bfloat16)],
+        compiler_params=pltpu.CompilerParams(vmem_limit_bytes=VMEM_BYTES),
         name="solve",
     )(packed, mode_variance.reshape(1, width), prior_mean.reshape(1, width))
 

time: 29.5 us -> 28 us (0.949)
  Pallas kernels: 28.6 us -> 24 us
  local copies, waits for them, and re-layouts: 0 us -> 3.06 us
    unnamed x0 -> x14, local copies, waits for them, and re-layouts: none -> 3.06 us
    pallas_call x1, Pallas kernels: 21.2 us -> 18.7 us  [shards(): pl.pallas_call(functools.partial(exchange, tm_size, sta_size, rows, half)...]
    pallas_call x1, Pallas kernels: 7.46 us -> 5.27 us  [shards(): pl.pallas_call(functools.partial(solve, tm_size, half), out_shape=jax.Sha...]
where the time goes in v2:
time: 28 us; the launch traced here: 27.7 us
  Pallas kernels  24 us (86%)
  local copies, waits for them, and re-layouts  3.06 us (11%)
  between operations  0.72 us (3%)
    pallas_call x1, Pallas kernels, shards(): pl.pallas_call(functools.partial(exchange, tm_size, sta_size, rows, half)...  18.7 us
    pallas_call x1, Pallas kernels, shards(): pl.pallas_call(functools.partial(solve, tm_size, half), out_shape=jax.Sha...  5.27 us
    unnamed x14, local copies, waits for them, and re-layouts  3.06 us

profile of v2, /device:TPU:0, one launch (start us, length us, event | category | flops | bytes accessed | tf_op | source)
XLA Modules:
  0.0 27.7 jit_solution(16480638551426268376)
XLA Ops:
  0.0 0.0 copy-start.1
  0.7 0.0 copy-start.3
  0.7 0.0 copy-start.6
  0.7 0.0 copy-done.1
  0.7 0.7 %copy-done.3 = f32[1,256]{1,0:T(1,128)S(1)} copy-done((f32[1,256]{1,0:T(1,128)S(1)}, f32[1,256]{1,0:T(1,128)}, u32[]{:S(2)}) %copy-start.3) | copy-done | bytes 1048
  1.3 0.0 copy-done.6
  1.4 0.0 copy-start
  1.4 1.0 %copy-done = bf16[1,1024,256]{2,1,0:T(8,128)(2,1)S(1)} copy-done((bf16[1,1024,256]{2,1,0:T(8,128)(2,1)S(1)}, bf16[1,1024,256]{2,1,0:T(8,128)(2,1)}, u32[]{:S(2)}) %copy-start) | copy-done | bytes 524312
  2.4 0.0 copy-start.2
  2.4 0.7 %copy-done.2 = s32[1,1024]{1,0:T(1,128)S(1)} copy-done((s32[1,1024]{1,0:T(1,128)S(1)}, s32[1,1024]{1,0:T(1,128)}, u32[]{:S(2)}) %copy-start.2) | copy-done | bytes 4120
  3.1 0.0 copy-start.5
  3.1 18.7 %exchange.1 = f32[4,8,40,128]{3,2,1,0:T(8,128)S(1)} custom-call(bf16[1,1024,256]{2,1,0:T(8,128)(2,1)S(1)} %copy-done, bf16[1,1024]{1,0:T(2,128)(2,1)S(1)} %copy-done.1, s32[1,1024]{1,0:T(1,128)S(1)} %copy-done.2, s32[1,1]{1,0:T(1,128)S(6)} %copy.9.count_ref, f32[16]{0:T(128)S(1)} %copy-done.6, f32[1,256]{1,0:T(1,128)S(1)} %copy-done.3), custom_call_target="tpu_custom_call" | custom-call | tf_op jit(solution)/shard_map/exchange/pallas_call | solution.py:343
  21.8 0.0 copy-start.4
  21.8 0.0 copy-done.5
  21.8 0.7 %copy-done.4 = f32[256]{0:T(256)S(1)} copy-done((f32[256]{0:T(256)S(1)}, f32[256]{0:T(256)}, u32[]{:S(2)}) %copy-start.4) | copy-done | bytes 1048
  22.5 5.3 %solve.1 = f32[1,256]{1,0:T(1,128)} custom-call(f32[4,320,128]{2,1,0:T(8,128)S(1)} %bitcast.3, f32[1,256]{1,0:T(1,128)S(1)} %bitcast.4, f32[1,256]{1,0:T(1,128)S(1)} %bitcast.5), custom_call_target="tpu_custom_call" | custom-call | tf_op jit(solution)/shard_map/solve/pallas_call | solution.py:364
Async XLA Ops:
  0.0 0.7 %copy-start.1 = (bf16[1,1024]{1,0:T(2,128)(2,1)S(1)}, bf16[1,1024]{1,0:T(2,128)(2,1)}, u32[]{:S(2)}) copy-start(bf16[1,1024]{1,0:T(2,128)(2,1)} %delay_ref.1) | copy-start | bytes 6148
  0.7 0.7 %copy-start.3 = (f32[1,256]{1,0:T(1,128)S(1)}, f32[1,256]{1,0:T(1,128)}, u32[]{:S(2)}) copy-start(f32[1,256]{1,0:T(1,128)} %decay_ref.1) | copy-start | bytes 3076
  0.7 0.7 %copy-start.6 = (f32[16]{0:T(128)S(1)}, f32[16]{0:T(128)}, u32[]{:S(2)}) copy-start(f32[16]{0:T(128)} %var_ref.1) | copy-start | bytes 196
  1.4 1.0 %copy-start = (bf16[1,1024,256]{2,1,0:T(8,128)(2,1)S(1)}, bf16[1,1024,256]{2,1,0:T(8,128)(2,1)}, u32[]{:S(2)}) copy-start(bf16[1,1024,256]{2,1,0:T(8,128)(2,1)} %basis_ref.1) | copy-start | bytes 1572868
  2.4 0.7 %copy-start.2 = (s32[1,1024]{1,0:T(1,128)S(1)}, s32[1,1024]{1,0:T(1,128)}, u32[]{:S(2)}) copy-start(s32[1,1024]{1,0:T(1,128)} %station_ref.1) | copy-start | bytes 12292
  3.1 18.7 %copy-start.5 = (f32[256]{0:T(256)S(1)}, f32[256]{0:T(256)}, u32[]{:S(2)}) copy-start(f32[256]{0:T(256)} %param.15) | copy-start | bytes 3076
  21.8 0.7 %copy-start.4 = (f32[256]{0:T(256)S(1)}, f32[256]{0:T(256)}, u32[]{:S(2)}) copy-start(f32[256]{0:T(256)} %param.14) | copy-start | bytes 3076

commit v3 on v2

--- a/solution.py
+++ b/solution.py
@@ -35,8 +35,9 @@
 
 def exchange(
     tm_size, sta_size, rows, half,
-    basis_ref, delay_ref, station_ref, count_ref, var_ref, decay_ref, out_ref,
-    part, landed, rs_send, rs_recv, z_send, plane_send, core_send, gather_recv,
+    basis_hbm, delay_hbm, station_hbm, count_hbm, var_hbm, decay_hbm, out_ref,
+    basis_ref, delay_ref, station_ref, count_ref, var_ref, decay_ref, load_sem,
+    part, landed, rs_send, rs_recv, z_send, plane_send, core_send, gather_recv, chain,
 ):
     tm = lax.axis_index("tm")
     sta = lax.axis_index("sta")
@@ -50,12 +51,37 @@
         peer = (sta + 1 + i) % sta_size
         pl.semaphore_signal(barrier, inc=1, device_id=(tm, peer), device_id_type=MESH)
 
-    def greet_column(i):
-        peer = (tm + 1 + i) % tm_size
-        pl.semaphore_signal(barrier, inc=1, device_id=(peer, sta), device_id_type=MESH)
-
+    has_below, has_above = tm > 0, tm < tm_size - 1
+
+    def to_neighbours(below_sem, above_sem):
+        @pl.when(has_below)
+        def _():
+            pl.semaphore_signal(
+                below_sem, inc=1, device_id=(tm - 1, sta), device_id_type=MESH
+            )
+
+        @pl.when(has_above)
+        def _():
+            pl.semaphore_signal(
+                above_sem, inc=1, device_id=(tm + 1, sta), device_id_type=MESH
+            )
+
+    to_neighbours(barrier, barrier)
     loop(sta_size - 1, greet_plane)
-    loop(tm_size - 1, greet_column)
+
+    loads = [
+        pltpu.make_async_copy(source, target, load_sem.at[i])
+        for i, (source, target) in enumerate(
+            (
+                (count_hbm, count_ref), (var_hbm, var_ref), (station_hbm, station_ref),
+                (basis_hbm, basis_ref), (delay_hbm, delay_ref), (decay_hbm, decay_ref),
+            )
+        )
+    ]
+    for load in loads:
+        load.start()
+    for load in loads:
+        load.wait()
 
     rays = basis_ref.shape[1]
     width = 2 * half
@@ -102,7 +128,9 @@
     for s in range(sta_size):
         part[s] = flat[s * rows : (s + 1) * rows]
 
-    pl.semaphore_wait(barrier, sta_size + tm_size - 2)
+    pl.semaphore_wait(
+        barrier, sta_size - 1 + has_below.astype(jnp.int32) + has_above.astype(jnp.int32)
+    )
 
     def scatter(i):
         peer = (sta + 1 + i) % sta_size
@@ -121,6 +149,19 @@
         )
 
     loop(sta_size - 1, lambda i: scatter(i).start())
+
+    def widen(i):
+        to_neighbours(chain.at[0], chain.at[1])
+
+        @pl.when(has_above)
+        def _():
+            pl.semaphore_wait(chain.at[0], 1)
+
+        @pl.when(has_below)
+        def _():
+            pl.semaphore_wait(chain.at[1], 1)
+
+    loop(tm_size - 2, widen)
     loop(sta_size - 1, lambda i: scattered(i).wait_recv())
     total = part[sta]
     if sta_size <= 16:
@@ -201,13 +242,21 @@
     return jnp.sum(acc, axis=1, keepdims=True)
 
 
-def solve(epochs, half, packed_ref, variance_ref, prior_ref, out_ref, table):
+def solve(
+    epochs, half, packed_ref, variance_hbm, prior_hbm, out_ref,
+    table, variance_ref, prior_ref, load_sem,
+):
+    loads = [
+        pltpu.make_async_copy(variance_hbm, variance_ref, load_sem.at[0]),
+        pltpu.make_async_copy(prior_hbm, prior_ref, load_sem.at[1]),
+    ]
+    for load in loads:
+        load.start()
     width = 2 * half
     tm = lax.axis_index("tm")
     row_id = lax.broadcasted_iota(jnp.int32, (half, half), 0)
     col_id = lax.broadcasted_iota(jnp.int32, (half, half), 1)
     diagonal = row_id == col_id
-    variance = variance_ref[...]
     decay, drive, info_diag = [], [], []
     for e in range(epochs):
         mixed = packed_ref[e, :half]
@@ -236,6 +285,9 @@
         )
         drive.append(jnp.concatenate([tail[1:2], tail[2:3]], axis=1))
         decay.append(jnp.concatenate([tail[3:4], tail[4:5]], axis=1))
+    for load in loads:
+        load.wait()
+    variance = variance_ref[...]
     inverse_noise = [1.0 / ((1.0 - d * d) * variance) for d in decay]
     off = [-decay[e] * inverse_noise[e] for e in range(epochs)]
     main = []
@@ -338,14 +390,21 @@
     rows = shard_rows(half, sta_size)
     chips = sta_size // CORES
     vmem = pl.BlockSpec(memory_space=pltpu.VMEM)
-    smem = pl.BlockSpec(memory_space=pltpu.SMEM)
+    hbm = pl.BlockSpec(memory_space=pltpu.HBM)
     dma = pltpu.SemaphoreType.DMA
     packed = pl.pallas_call(
         functools.partial(exchange, tm_size, sta_size, rows, half),
         out_shape=jax.ShapeDtypeStruct((tm_size, sta_size, rows, half), jnp.float32),
-        in_specs=[vmem, vmem, vmem, smem, smem, vmem],
+        in_specs=[hbm] * 6,
         out_specs=vmem,
         scratch_shapes=[
+            pltpu.VMEM(ray_basis.shape, ray_basis.dtype),
+            pltpu.VMEM(delays.shape, delays.dtype),
+            pltpu.VMEM(ray_station.shape, ray_station.dtype),
+            pltpu.SMEM(ray_count.shape, ray_count.dtype),
+            pltpu.SMEM(station_var.shape, station_var.dtype),
+            pltpu.VMEM(decay_factor.shape, decay_factor.dtype),
+            dma((6,)),
             pltpu.VMEM((sta_size, rows, half), jnp.float32),
             pltpu.VMEM((sta_size, rows, half), jnp.float32),
             dma((sta_size - 1,)),
@@ -354,22 +413,36 @@
             dma((tm_size, chips - 1)),
             dma((tm_size, chips)),
             dma((tm_size, sta_size)),
+            pltpu.SemaphoreType.REGULAR((2,)),
         ],
         compiler_params=pltpu.CompilerParams(
             collective_id=0, has_side_effects=True, vmem_limit_bytes=VMEM_BYTES
         ),
         name="exchange",
-    )(ray_basis, delays, ray_station, ray_count, station_var, decay_factor)
+    )(*[
+        pltpu.with_memory_space_constraint(x, pltpu.HBM)
+        for x in (ray_basis, delays, ray_station)
+    ], ray_count, *[
+        pltpu.with_memory_space_constraint(x, pltpu.HBM) for x in (station_var, decay_factor)
+    ])
     packed = packed.reshape(tm_size, sta_size * rows, half)
     return pl.pallas_call(
         functools.partial(solve, tm_size, half),
         out_shape=jax.ShapeDtypeStruct((1, width), jnp.float32),
-        in_specs=[vmem, vmem, vmem],
+        in_specs=[vmem, hbm, hbm],
         out_specs=vmem,
-        scratch_shapes=[pltpu.VMEM((tm_size, 2 * width, width), jnp.bfloat16)],
+        scratch_shapes=[
+            pltpu.VMEM((tm_size, 2 * width, width), jnp.bfloat16),
+            pltpu.VMEM((1, width), jnp.float32),
+            pltpu.VMEM((1, width), jnp.float32),
+            dma((2,)),
+        ],
         compiler_params=pltpu.CompilerParams(vmem_limit_bytes=VMEM_BYTES),
         name="solve",
-    )(packed, mode_variance.reshape(1, width), prior_mean.reshape(1, width))
+    )(packed, *[
+        pltpu.with_memory_space_constraint(x.reshape(1, width), pltpu.HBM)
+        for x in (mode_variance, prior_mean)
+    ])
 
 
 def solution(mesh):

time: 28 us -> 24.9 us (0.89)
  local copies, waits for them, and re-layouts: 3.06 us -> 0 us
    unnamed x14 -> x0, local copies, waits for them, and re-layouts: 3.06 us -> none
    pallas_call x1, Pallas kernels: 5.27 us -> 5.85 us  [shards(): pl.pallas_call(functools.partial(solve, tm_size, half), out_shape=jax.Sha...]
    pallas_call x1, Pallas kernels: 18.7 us -> 18.2 us  [shards(): pl.pallas_call(functools.partial(exchange, tm_size, sta_size, rows, half)...]
where the time goes in v3:
time: 24.9 us; the launch traced here: 24.7 us
  Pallas kernels  24.1 us (97%)
  between operations  0.66 us (3%)
    pallas_call x1, Pallas kernels, shards(): pl.pallas_call(functools.partial(exchange, tm_size, sta_size, rows, half)...  18.2 us
    pallas_call x1, Pallas kernels, shards(): pl.pallas_call(functools.partial(solve, tm_size, half), out_shape=jax.Sha...  5.85 us

profile of v3, /device:TPU:0, one launch (start us, length us, event | category | flops | bytes accessed | tf_op | source)
XLA Modules:
  0.0 24.7 jit_solution(11177702102631724720)
XLA Ops:
  0.7 18.2 %exchange.1 = f32[4,8,40,128]{3,2,1,0:T(8,128)S(1)} custom-call(bf16[1,1024,256]{2,1,0:T(8,128)(2,1)} %basis_hbm.1, bf16[1,1024]{1,0:T(2,128)(2,1)} %delay_hbm.1, s32[1,1024]{1,0:T(1,128)} %station_hbm.1, s32[1,1]{1,0:T(1,128)S(6)} %copy.9.count_hbm, f32[16]{0:T(128)} %var_hbm.1, f32[1,256]{1,0:T(1,128)} %decay_hbm.1), custom_call_target="tpu_custom_call" | custom-call | tf_op jit(solution)/shard_map/exchange/pallas_call | solution.py:395
  18.9 5.8 %solve.1 = f32[1,256]{1,0:T(1,128)} custom-call(f32[4,320,128]{2,1,0:T(8,128)S(1)} %bitcast.3, f32[1,256]{1,0:T(1,128)} %bitcast.4, f32[1,256]{1,0:T(1,128)} %bitcast.5), custom_call_target="tpu_custom_call" | custom-call | tf_op jit(solution)/shard_map/solve/pallas_call | solution.py:429

commit v4 on v3

--- a/solution.py
+++ b/solution.py
@@ -35,8 +35,9 @@
 
 def exchange(
     tm_size, sta_size, rows, half,
-    basis_hbm, delay_hbm, station_hbm, count_hbm, var_hbm, decay_hbm, out_ref,
-    basis_ref, delay_ref, station_ref, count_ref, var_ref, decay_ref, load_sem,
+    basis_hbm, delay_hbm, station_hbm, count_ref, var_hbm, decay_hbm, variance_hbm, prior_hbm,
+    out_ref, variance_ref, prior_ref,
+    basis_ref, delay_ref, station_ref, var_ref, decay_ref, load_sem,
     part, landed, rs_send, rs_recv, z_send, plane_send, core_send, gather_recv, chain,
 ):
     tm = lax.axis_index("tm")
@@ -73,8 +74,9 @@
         pltpu.make_async_copy(source, target, load_sem.at[i])
         for i, (source, target) in enumerate(
             (
-                (count_hbm, count_ref), (var_hbm, var_ref), (station_hbm, station_ref),
+                (var_hbm, var_ref), (station_hbm, station_ref),
                 (basis_hbm, basis_ref), (delay_hbm, delay_ref), (decay_hbm, decay_ref),
+                (variance_hbm, variance_ref), (prior_hbm, prior_ref),
             )
         )
     ]
@@ -91,7 +93,7 @@
     noise = jnp.ones((1, rays), jnp.float32)
     for s in range(var_ref.shape[0]):
         noise = jnp.where(local == s, var_ref[s], noise)
-    weight = jnp.where(slots < count_ref[0, 0], 1.0 / noise, 0.0)
+    weight = jnp.where(slots < count_ref[...], 1.0 / noise, 0.0)
     square = jnp.concatenate(
         [weight[:, g * 128 : (g + 1) * 128] for g in range(groups)]
         + [jnp.zeros((128 - groups, 128), jnp.float32)],
@@ -242,16 +244,7 @@
     return jnp.sum(acc, axis=1, keepdims=True)
 
 
-def solve(
-    epochs, half, packed_ref, variance_hbm, prior_hbm, out_ref,
-    table, variance_ref, prior_ref, load_sem,
-):
-    loads = [
-        pltpu.make_async_copy(variance_hbm, variance_ref, load_sem.at[0]),
-        pltpu.make_async_copy(prior_hbm, prior_ref, load_sem.at[1]),
-    ]
-    for load in loads:
-        load.start()
+def solve(epochs, half, packed_ref, variance_ref, prior_ref, out_ref, table):
     width = 2 * half
     tm = lax.axis_index("tm")
     row_id = lax.broadcasted_iota(jnp.int32, (half, half), 0)
@@ -285,8 +278,6 @@
         )
         drive.append(jnp.concatenate([tail[1:2], tail[2:3]], axis=1))
         decay.append(jnp.concatenate([tail[3:4], tail[4:5]], axis=1))
-    for load in loads:
-        load.wait()
     variance = variance_ref[...]
     inverse_noise = [1.0 / ((1.0 - d * d) * variance) for d in decay]
     off = [-decay[e] * inverse_noise[e] for e in range(epochs)]
@@ -392,19 +383,22 @@
     vmem = pl.BlockSpec(memory_space=pltpu.VMEM)
     hbm = pl.BlockSpec(memory_space=pltpu.HBM)
     dma = pltpu.SemaphoreType.DMA
-    packed = pl.pallas_call(
+    packed, variance, prior = pl.pallas_call(
         functools.partial(exchange, tm_size, sta_size, rows, half),
-        out_shape=jax.ShapeDtypeStruct((tm_size, sta_size, rows, half), jnp.float32),
-        in_specs=[hbm] * 6,
-        out_specs=vmem,
+        out_shape=(
+            jax.ShapeDtypeStruct((tm_size, sta_size, rows, half), jnp.float32),
+            jax.ShapeDtypeStruct((1, width), jnp.float32),
+            jax.ShapeDtypeStruct((1, width), jnp.float32),
+        ),
+        in_specs=[hbm, hbm, hbm, vmem, hbm, hbm, hbm, hbm],
+        out_specs=(vmem, vmem, vmem),
         scratch_shapes=[
             pltpu.VMEM(ray_basis.shape, ray_basis.dtype),
             pltpu.VMEM(delays.shape, delays.dtype),
             pltpu.VMEM(ray_station.shape, ray_station.dtype),
-            pltpu.SMEM(ray_count.shape, ray_count.dtype),
             pltpu.SMEM(station_var.shape, station_var.dtype),
             pltpu.VMEM(decay_factor.shape, decay_factor.dtype),
-            dma((6,)),
+            dma((7,)),
             pltpu.VMEM((sta_size, rows, half), jnp.float32),
             pltpu.VMEM((sta_size, rows, half), jnp.float32),
             dma((sta_size - 1,)),
@@ -423,26 +417,23 @@
         pltpu.with_memory_space_constraint(x, pltpu.HBM)
         for x in (ray_basis, delays, ray_station)
     ], ray_count, *[
-        pltpu.with_memory_space_constraint(x, pltpu.HBM) for x in (station_var, decay_factor)
+        pltpu.with_memory_space_constraint(x, pltpu.HBM) for x in (
+            station_var, decay_factor,
+            mode_variance.reshape(1, width), prior_mean.reshape(1, width),
+        )
     ])
     packed = packed.reshape(tm_size, sta_size * rows, half)
     return pl.pallas_call(
         functools.partial(solve, tm_size, half),
         out_shape=jax.ShapeDtypeStruct((1, width), jnp.float32),
-        in_specs=[vmem, hbm, hbm],
+        in_specs=[vmem, vmem, vmem],
         out_specs=vmem,
         scratch_shapes=[
             pltpu.VMEM((tm_size, 2 * width, width), jnp.bfloat16),
-            pltpu.VMEM((1, width), jnp.float32),
-            pltpu.VMEM((1, width), jnp.float32),
-            dma((2,)),
         ],
         compiler_params=pltpu.CompilerParams(vmem_limit_bytes=VMEM_BYTES),
         name="solve",
-    )(packed, *[
-        pltpu.with_memory_space_constraint(x.reshape(1, width), pltpu.HBM)
-        for x in (mode_variance, prior_mean)
-    ])
+    )(packed, variance, prior)
 
 
 def solution(mesh):

time: 24.9 us -> 24.3 us (0.976)
  Pallas kernels: 24.1 us -> 23.5 us
    pallas_call x1, Pallas kernels: 5.85 us -> 5.24 us  [shards(): pl.pallas_call(functools.partial(solve, tm_size, half), out_shape=jax.Sha...]
where the time goes in v4:
time: 24.3 us; the launch traced here: 24.1 us
  Pallas kernels  23.5 us (97%)
  between operations  0.66 us (3%)
    pallas_call x1, Pallas kernels, shards(): pl.pallas_call(functools.partial(exchange, tm_size, sta_size, rows, half)...  18.2 us
    pallas_call x1, Pallas kernels, shards(): pl.pallas_call(functools.partial(solve, tm_size, half), out_shape=jax.Sha...  5.24 us

profile of v4, /device:TPU:0, one launch (start us, length us, event | category | flops | bytes accessed | tf_op | source)
XLA Modules:
  0.0 24.1 jit_solution(9217364115978636487)
XLA Ops:
  0.7 18.2 %exchange.1 = (f32[4,8,40,128]{3,2,1,0:T(8,128)S(1)}, f32[1,256]{1,0:T(1,128)S(1)}, f32[1,256]{1,0:T(1,128)S(1)}) custom-call(bf16[1,1024,256]{2,1,0:T(8,128)(2,1)} %basis_hbm.1, bf16[1,1024]{1,0:T(2,128)(2,1)} %delay_hbm.1, s32[1,1024]{1,0:T(1,128)} %station_hbm.1, s32[1,1]{1,0:T(1,128)S(6)} %copy.9.count_ref, f32[16]{0:T(128)} %var_hbm.1, ...), custom_call_target="tpu_custom_call" | custom-call | tf_op jit(solution)/shard_map/exchange/pallas_call | solution.py:386
  18.9 5.2 %solve.1 = f32[1,256]{1,0:T(1,128)} custom-call(f32[4,320,128]{2,1,0:T(8,128)S(1)} %bitcast.3, f32[1,256]{1,0:T(1,128)S(1)} %get-tuple-element.9.variance_ref, f32[1,256]{1,0:T(1,128)S(1)} %get-tuple-element.10.prior_ref), custom_call_target="tpu_custom_call" | custom-call | tf_op jit(solution)/shard_map/solve/pallas_call | solution.py:426

commit v5 on v4

--- a/solution.py
+++ b/solution.py
@@ -351,6 +351,27 @@
             rz = new
         return tuple(x), tuple(r), tuple(p), rz
 
+    def opening(x, r, u, gamma):
+        w = apply(u)
+        alpha = gamma / jnp.maximum(total_of([a * b for a, b in zip(u, w)]), tiny)
+        p, s = u, w
+        for step in range(FIRST_STEPS):
+            x = [a + alpha * b for a, b in zip(x, p)]
+            r = [a - alpha * b for a, b in zip(r, s)]
+            u = precondition(r)
+            new = total_of([a * b for a, b in zip(r, u)])
+            if step + 1 < FIRST_STEPS:
+                w = apply(u)
+                delta = total_of([a * b for a, b in zip(u, w)])
+                beta = new / jnp.maximum(gamma, tiny)
+                bend = delta - beta * new / jnp.maximum(alpha, tiny)
+                bend = jnp.maximum(bend, jnp.maximum(1e-3 * delta, tiny))
+                alpha = new / bend
+                p = [a + beta * b for a, b in zip(u, p)]
+                s = [a + beta * b for a, b in zip(w, s)]
+            gamma = new
+        return tuple(x), tuple(r), tuple(u), gamma
+
     def going(rz):
         return jnp.max((rz > goal).astype(jnp.int32)) > 0
 
@@ -359,7 +380,7 @@
         state = advance(state, STEPS_PER_CHECK)
         return count + 1, going(state[3]), state
 
-    state = advance((zero, target, first_z, first_rz), FIRST_STEPS)
+    state = opening(zero, target, first_z, first_rz)
     final = lax.while_loop(
         lambda c: jnp.logical_and(c[1], c[0] < MAX_CHECKS),
         body,

time: 24.3 us -> 23.8 us (0.979)
  Pallas kernels: 23.5 us -> 23 us
    pallas_call x1, Pallas kernels: 5.24 us -> 4.74 us  [shards(): pl.pallas_call(functools.partial(solve, tm_size, half), out_shape=jax.Sha...]
where the time goes in v5:
time: 23.8 us; the launch traced here: 23.6 us
  Pallas kernels  23 us (97%)
  between operations  0.66 us (3%)
    pallas_call x1, Pallas kernels, shards(): pl.pallas_call(functools.partial(exchange, tm_size, sta_size, rows, half)...  18.2 us
    pallas_call x1, Pallas kernels, shards(): pl.pallas_call(functools.partial(solve, tm_size, half), out_shape=jax.Sha...  4.74 us

profile of v5, /device:TPU:0, one launch (start us, length us, event | category | flops | bytes accessed | tf_op | source)
XLA Modules:
  0.0 23.6 jit_solution(5657138520772526480)
XLA Ops:
  0.7 18.2 %exchange.1 = (f32[4,8,40,128]{3,2,1,0:T(8,128)S(1)}, f32[1,256]{1,0:T(1,128)S(1)}, f32[1,256]{1,0:T(1,128)S(1)}) custom-call(bf16[1,1024,256]{2,1,0:T(8,128)(2,1)} %basis_hbm.1, bf16[1,1024]{1,0:T(2,128)(2,1)} %delay_hbm.1, s32[1,1024]{1,0:T(1,128)} %station_hbm.1, s32[1,1]{1,0:T(1,128)S(6)} %copy.9.count_ref, f32[16]{0:T(128)} %var_hbm.1, ...), custom_call_target="tpu_custom_call" | custom-call | tf_op jit(solution)/shard_map/exchange/pallas_call | solution.py:407
  18.9 4.7 %solve.1 = f32[1,256]{1,0:T(1,128)} custom-call(f32[4,320,128]{2,1,0:T(8,128)S(1)} %bitcast.3, f32[1,256]{1,0:T(1,128)S(1)} %get-tuple-element.9.variance_ref, f32[1,256]{1,0:T(1,128)S(1)} %get-tuple-element.10.prior_ref), custom_call_target="tpu_custom_call" | custom-call | tf_op jit(solution)/shard_map/solve/pallas_call | solution.py:447

commit v6 on v5

--- a/solution.py
+++ b/solution.py
@@ -298,7 +298,7 @@
             pivot = pivot - ratio[-1] * off[e]
         pivot_inverse.append(1.0 / pivot)
 
-    def precondition(r):
+    def eliminate(r):
         y = [r[0]]
         for e in range(1, epochs):
             y.append(r[e] - ratio[e - 1] * y[-1])
@@ -306,6 +306,24 @@
         z[-1] = y[-1] * pivot_inverse[-1]
         for e in range(epochs - 2, -1, -1):
             z[e] = y[e] * pivot_inverse[e] - ratio[e] * z[e + 1]
+        return z
+
+    if epochs <= 8:
+        ones = jnp.ones((1, width), jnp.float32)
+        units = [
+            eliminate([ones if e == f else jnp.zeros_like(ones) for e in range(epochs)])
+            for f in range(epochs)
+        ]
+
+    def precondition(r):
+        if epochs > 8:
+            return eliminate(r)
+        z = []
+        for e in range(epochs):
+            terms = [units[f][e] * r[f] for f in range(epochs)]
+            while len(terms) > 1:
+                terms = [sum(terms[i : i + 2][1:], terms[i]) for i in range(0, len(terms), 2)]
+            z.append(terms[0])
         return z
 
     pick = lax.broadcasted_iota(jnp.int32, (8, width), 0)

time: 23.8 us -> 24.4 us (1.025)
  Pallas kernels: 23 us -> 23.5 us
    pallas_call x1, Pallas kernels: 4.74 us -> 5.3 us  [shards(): pl.pallas_call(functools.partial(solve, tm_size, half), out_shape=jax.Sha...]
where the time goes in v6:
time: 24.4 us; the launch traced here: 24.2 us
  Pallas kernels  23.5 us (96%)
  between operations  0.66 us (3%)
    pallas_call x1, Pallas kernels, shards(): pl.pallas_call(functools.partial(exchange, tm_size, sta_size, rows, half)...  18.2 us
    pallas_call x1, Pallas kernels, shards(): pl.pallas_call(functools.partial(solve, tm_size, half), out_shape=jax.Sha...  5.3 us

profile of v6, /device:TPU:0, one launch (start us, length us, event | category | flops | bytes accessed | tf_op | source)
XLA Modules:
  0.0 24.2 jit_solution(6191667097987810839)
XLA Ops:
  0.7 18.2 %exchange.1 = (f32[4,8,40,128]{3,2,1,0:T(8,128)S(1)}, f32[1,256]{1,0:T(1,128)S(1)}, f32[1,256]{1,0:T(1,128)S(1)}) custom-call(bf16[1,1024,256]{2,1,0:T(8,128)(2,1)} %basis_hbm.1, bf16[1,1024]{1,0:T(2,128)(2,1)} %delay_hbm.1, s32[1,1024]{1,0:T(1,128)} %station_hbm.1, s32[1,1]{1,0:T(1,128)S(6)} %copy.9.count_ref, f32[16]{0:T(128)} %var_hbm.1, ...), custom_call_target="tpu_custom_call" | custom-call | tf_op jit(solution)/shard_map/exchange/pallas_call | solution.py:425
  18.9 5.3 %solve.1 = f32[1,256]{1,0:T(1,128)} custom-call(f32[4,320,128]{2,1,0:T(8,128)S(1)} %bitcast.3, f32[1,256]{1,0:T(1,128)S(1)} %get-tuple-element.9.variance_ref, f32[1,256]{1,0:T(1,128)S(1)} %get-tuple-element.10.prior_ref), custom_call_target="tpu_custom_call" | custom-call | tf_op jit(solution)/shard_map/solve/pallas_call | solution.py:465
